TPU v7x, 512 devices: a whole 4x4x16 slice. The times are simulated.
512 devices in a mesh: row: 32 (over y, z_hi, x), col: 16 (over z_lo, core).
Axes of the slice: x: 4, y: 4, z: 16 (z_hi: 2, z_lo: 8; z = z_hi * 8 + z_lo), core: 2. Of those that a mesh axis runs over, the one named last changes fastest.
Arguments:
- query_field: bfloat16 [512, 256, 1152], P('row', 'col'), may hold values from -136 to 136
- key_field: bfloat16 [512, 256, 1152], P('row', 'col'), may hold values from -8.5 to 8.5
- value_field: bfloat16 [512, 256, 1152], P('row', 'col'), may hold values from -6 to 6
- query_tan: bfloat16 [512, 256, 1152], P('row', 'col'), may hold values from -6 to 6
- key_tan: bfloat16 [512, 256, 1152], P('row', 'col'), may hold values from -6 to 6
- value_tan: bfloat16 [512, 256, 1152], P('row', 'col'), may hold values from -6 to 6
- pool_near: float32 [4, 4], replicated, may hold values from -1.5 to 1.5
- pool_far: float32 [16, 16], replicated, may hold values from -0.375 to 0.375
- level_bias: float32 [2, 16], replicated, may hold values from 0.5 to 2.5
Outputs:
- mixed: bfloat16 [512, 256, 1152], P('row', 'col')
- mixed_tan: bfloat16 [512, 256, 1152], P('row', 'col')
All inputs are finite; a program needn't handle non-finite values.
Results may differ from a plain program's by a relative error of at most 0.012.
Values may be sent and summed in bfloat16 or wider, within the bound.
A program may use at most 128 MiB of HBM per device.

v0:
```python
import jax
import jax.numpy as jnp
from jax import lax
from jax.sharding import PartitionSpec as P

HEADS = 16
RIM = 8
NEAR_POOL = 4


def with_halo(cells, sides, width):
    for axis, dim in sides:
        count = lax.axis_size(axis)
        ends = count - 1
        head = lax.slice_in_dim(cells, 0, width, axis=dim)
        tail = lax.slice_in_dim(cells, cells.shape[dim] - width, cells.shape[dim], axis=dim)
        cells = jnp.concatenate(
            [
                lax.ppermute(tail, axis, [(i, (i + 1) % count) for i in range(ends)]),
                cells,
                lax.ppermute(head, axis, [((i + 1) % count, i) for i in range(ends)]),
            ],
            axis=dim,
        )
    return cells


def partner(block, axis, stride):
    count = lax.axis_size(axis)
    route = []
    for low in range(count):
        high = low | 1 << stride
        if high != low and high < count:
            route += [(low, high), (high, low)]
    return lax.ppermute(block, axis, route)


def pool_stack(stacked_wide, weights, size):
    count, row_count, col_count, width = stacked_wide.shape
    blocks = stacked_wide.reshape(count, row_count // size, size, col_count // size, size, width)
    pooled = jnp.einsum("napbqd,pq->nabd", blocks, weights, precision=lax.Precision.HIGHEST)
    return pooled.astype(jnp.bfloat16).reshape(count, -1, width)


def body(
    query_field,
    key_field,
    value_field,
    query_tan,
    key_tan,
    value_tan,
    pool_near,
    pool_far,
    level_bias,
):
    window = query_field.shape[0]
    width = query_field.shape[2]
    head_dim = width // HEADS
    pair_width = 2 * head_dim
    token_count = window * window
    score_scale = head_dim ** (-0.5)
    stacked = jnp.stack([key_field, value_field, key_tan, value_tan], 0)
    extended = with_halo(stacked, (("row", 1), ("col", 2)), RIM)
    span = window + 2 * RIM
    fine_keys = extended.reshape(4, span * span, width)
    stacked_wide = stacked.astype(jnp.float32)
    near_local = pool_stack(stacked_wide, pool_near, NEAR_POOL)
    near_pair = jnp.concatenate([near_local, partner(near_local, "row", 0)], axis=1)
    near_keys = jnp.concatenate([near_pair, partner(near_pair, "col", 0)], axis=1)
    far_local = pool_stack(stacked_wide, pool_far, window)
    col_done = lax.all_gather(far_local, "col", axis=1, tiled=True)
    far_keys = lax.all_gather(col_done, "row", axis=1, tiled=True)
    row_ids = lax.axis_index("row") * window - RIM + jnp.arange(span, dtype=jnp.int32)
    col_ids = lax.axis_index("col") * window - RIM + jnp.arange(span, dtype=jnp.int32)
    row_ok = (row_ids >= 0) & (row_ids < window * lax.axis_size("row"))
    col_ok = (col_ids >= 0) & (col_ids < window * lax.axis_size("col"))
    valid = (row_ok[:, None] & col_ok[None, :]).reshape(span * span)
    query_flat = query_field.reshape(token_count, width)
    qtan_flat = query_tan.reshape(token_count, width)
    blocks = (fine_keys, near_keys, far_keys)

    def pair_step(group, carry):
        out_acc, tan_acc = carry
        start = group * pair_width

        def columns(array):
            return lax.dynamic_slice_in_dim(array, start, pair_width, array.ndim - 1)

        query_pair = columns(query_flat).reshape(token_count, 2, head_dim)
        qtan_pair = columns(qtan_flat).reshape(token_count, 2, head_dim)
        bias_pair = lax.dynamic_slice_in_dim(level_bias, group * 2, 2, 1)
        score_parts = []
        tangent_parts = []
        value_parts = []
        valtan_parts = []
        for level, block in enumerate(blocks):
            count = block.shape[1]
            key_part = columns(block[0]).reshape(count, 2, head_dim)
            keytan_part = columns(block[2]).reshape(count, 2, head_dim)
            value_parts.append(columns(block[1]).reshape(count, 2, head_dim))
            valtan_parts.append(columns(block[3]).reshape(count, 2, head_dim))
            level_scores = (
                jnp.einsum("qhd,khd->hqk", query_pair, key_part, preferred_element_type=jnp.float32)
                * score_scale
            )
            if level == 0:
                level_scores = jnp.where(valid[None, None, :], level_scores, jnp.float32(-jnp.inf))
            else:
                level_scores = level_scores + bias_pair[level - 1][:, None, None]
            score_parts.append(level_scores)
            tangent_parts.append(
                (
                    jnp.einsum(
                        "qhd,khd->hqk", qtan_pair, key_part, preferred_element_type=jnp.float32
                    )
                    + jnp.einsum(
                        "qhd,khd->hqk", query_pair, keytan_part, preferred_element_type=jnp.float32
                    )
                )
                * score_scale
            )
        top = jnp.max(score_parts[0], axis=-1, keepdims=True)
        for level in range(1, 3):
            top = jnp.maximum(top, jnp.max(score_parts[level], axis=-1, keepdims=True))
        total = jnp.zeros_like(top)
        for level in range(3):
            total = total + jnp.sum(jnp.exp(score_parts[level] - top), axis=-1, keepdims=True)
        row_total = jnp.zeros((2, token_count), jnp.float32)
        mix = jnp.zeros((token_count, 2, head_dim), jnp.float32)
        mix_extra = jnp.zeros((token_count, 2, head_dim), jnp.float32)
        for level in range(3):
            weights = jnp.exp(score_parts[level] - top) / total
            product = weights * tangent_parts[level]
            row_total = row_total + jnp.sum(product, axis=-1)
            weight_part = weights.astype(jnp.bfloat16)
            product_part = product.astype(jnp.bfloat16)
            mix = mix + jnp.einsum(
                "hqk,khd->qhd", weight_part, value_parts[level], preferred_element_type=jnp.float32
            )
            mix_extra = mix_extra + jnp.einsum(
                "hqk,khd->qhd", product_part, value_parts[level], preferred_element_type=jnp.float32
            )
            mix_extra = mix_extra + jnp.einsum(
                "hqk,khd->qhd", weight_part, valtan_parts[level], preferred_element_type=jnp.float32
            )
        mix_tan = mix_extra - jnp.transpose(row_total)[:, :, None] * mix
        out_acc = lax.dynamic_update_slice_in_dim(
            out_acc, mix.reshape(token_count, pair_width).astype(jnp.bfloat16), start, 1
        )
        tan_acc = lax.dynamic_update_slice_in_dim(
            tan_acc, mix_tan.reshape(token_count, pair_width).astype(jnp.bfloat16), start, 1
        )
        return (out_acc, tan_acc)

    empty = jnp.zeros((token_count, width), jnp.bfloat16)
    mixed, mixed_tan = lax.fori_loop(0, HEADS // 2, pair_step, (empty, empty))
    return (mixed.reshape(window, window, width), mixed_tan.reshape(window, window, width))


def solution(mesh):
    in_specs = (
        P("row", "col", None),
        P("row", "col", None),
        P("row", "col", None),
        P("row", "col", None),
        P("row", "col", None),
        P("row", "col", None),
        P(),
        P(),
        P(),
    )
    out_specs = (P("row", "col", None), P("row", "col", None))
    return jax.shard_map(body, mesh=mesh, in_specs=in_specs, out_specs=out_specs, check_vma=False)
```

profile of v0, /device:TPU:96, one launch (start us, length us, event | category | flops | bytes accessed | tf_op | source)
XLA Modules:
  0.0 478.5 jit_solution(2326812249168049933)
XLA Ops:
  7.2 2.0 pad_maximum_fusion.2
  9.2 1.7 fusion.56
  10.9 4.6 collective-permute-start
  17.8 21.2 %all-gather = bf16[4,18432]{1,0:T(4,128)(2,1)S(1)} all-gather(bf16[4,1152]{1,0:T(4,128)(2,1)S(1)} %bitcast.210), channel_id=2, replica_groups=mesh['row'=32,'col'=16] {'col'}, dimensions={1}, use_global_device_ids=true | all-gather | bytes 156672 | tf_op jit(solution)/shard_map/all_gather | solution.py:71
  39.9 5.1 %collective-permute-done.1 = bf16[4,8,16,1152]{3,2,1,0:T(8,128)(2,1)} collective-permute-done((bf16[4,8,16,1152]{3,2,1,0:T(8,128)(2,1)}, bf16[4,8,16,1152]{3,2,1,0:T(8,128)(2,1)}, u32[]{:S(2)}, u32[]{:S(2)}) %collective-permute-start.1) | collective-permute-done | bytes 1179680 | tf_op jit(solution)/shard_map/ppermute | solution.py:21
  45.1 2.8 pad_maximum_fusion.1
  47.9 2.6 fusion.55
  50.5 1.9 collective-permute-start.2
  52.5 3.7 collective-permute-start.3
  58.4 3.6 fusion.44
  62.1 4.6 collective-permute-start.4
  66.8 4.4 collective-permute-done.4
  71.2 2.1 collective-permute-start.5
  74.6 2.1 copy.25
  77.9 3.2 collective-permute-done.2
  81.1 1.8 collective-permute-done.3
  82.9 9.8 %pad_maximum_fusion = bf16[4,32,32,1152]{3,2,1,0:T(8,128)(2,1)} fusion(bf16[4,32,8,1152]{3,2,1,0:T(8,128)(2,1)} %collective-permute-done.3, bf16[4,8,16,1152]{3,2,1,0:T(8,128)(2,1)} %collective-permute-done.1, bf16[1,16,16,1152]{3,2,1,0:T(8,128)(2,1)S(1)} %bitcast.188, bf16[1,16,16,1152]{3,2,1,0:T(8,128)(2,1)S(1)} %bitcast.191, ...), kind=kLoop, calls=%fused_computation.75 | loop fusion | flops 75497472 | bytes 18874368 | tf_op jit(solution)/shard_map/concatenate | solution.py:17
  92.6 12.6 %copy.22 = bf16[4,1024,1152]{1,2,0:T(8,128)(2,1)} copy(bf16[4,1024,1152]{2,1,0:T(8,128)(2,1)} %bitcast.169) | data formatting | bytes 18874368
  105.3 228.3 %all-gather.3.cloned.1.call-done = bf16[4,512,1152]{2,1,0:T(8,128)(2,1)} async-done(((bf16[4,16,1152]{2,1,0:T(8,128)(2,1)}), bf16[4,512,1152]{2,1,0:T(8,128)(2,1)}) %all-gather.3.cloned.1.call-update) | async-done | bytes 4718608 | tf_op jit(solution)/shard_map/all_gather | solution.py:72
  333.5 6.7 %copy.24 = bf16[4,512,1152]{1,2,0:T(8,128)(2,1)} copy(bf16[4,512,1152]{2,1,0:T(8,128)(2,1)} %all-gather.3.cloned.1.call-done) | data formatting | bytes 9437184
  340.3 129.2 %while.16 = (s32[]{:T(128)}, bf16[256,1152]{0,1:T(8,128)(2,1)S(1)}, bf16[256,1152]{0,1:T(8,128)(2,1)S(1)}, bf16[4,1024,1152]{1,2,0:T(8,128)(2,1)}, bf16[256,1152...) while((s32[]{:T(128)}, bf16[256,1152]{0,1:T(8,128)(2,1)S(1)}, ...), condition=%wide.region_10.11_spmd.clone, body=%wide.region_0.10_spmd.clone.sunk | while | flops 726347264 | bytes 104430016 | solution.py:156
  342.6 2.8 fusion.181
  346.3 1.4 copy-done.2
  358.7 2.8 fusion.181
  374.9 2.8 fusion.181
  378.6 1.4 copy-done.2
  391.0 2.8 fusion.181
  394.7 1.4 copy-done.2
  407.2 2.8 fusion.181
  423.3 2.8 fusion.181
  439.5 2.8 fusion.181
  455.6 2.8 fusion.181
  (455 shorter events, 111.3 us)
Async XLA Ops:
  7.2 9.6 %copy-start = (f32[16,16]{1,0:T(8,128)S(1)}, f32[16,16]{1,0:T(8,128)}, u32[]{:S(2)}) copy-start(f32[16,16]{1,0:T(8,128)} %param.18) | copy-start | bytes 3076
  7.2 326.3 %all-gather.3.cloned.1.call-start = ((), (), s32[]{:S(2)}) async-start(), calls=%async_computation | async-start | bytes 4866048 | tf_op jit(solution)/shard_map/all_gather | solution.py:72
  10.8 34.2 %copy-start.3 = (bf16[16,16,1152]{2,1,0:T(8,128)(2,1)S(1)}, bf16[16,16,1152]{2,1,0:T(8,128)(2,1)}, u32[]{:S(2)}) copy-start(bf16[16,16,1152]{2,1,0:T(8,128)(2,1)} %param.16) | copy-start | bytes 1769476
  10.8 34.2 %copy-start.4 = (bf16[16,16,1152]{2,1,0:T(8,128)(2,1)S(1)}, bf16[16,16,1152]{2,1,0:T(8,128)(2,1)}, u32[]{:S(2)}) copy-start(bf16[16,16,1152]{2,1,0:T(8,128)(2,1)} %param.15) | copy-start | bytes 1769476
  10.9 34.2 %copy-start.5 = (bf16[16,16,1152]{2,1,0:T(8,128)(2,1)S(1)}, bf16[16,16,1152]{2,1,0:T(8,128)(2,1)}, u32[]{:S(2)}) copy-start(bf16[16,16,1152]{2,1,0:T(8,128)(2,1)} %param.13) | copy-start | bytes 1769476
  10.9 34.2 %copy-start.6 = (bf16[16,16,1152]{2,1,0:T(8,128)(2,1)S(1)}, bf16[16,16,1152]{2,1,0:T(8,128)(2,1)}, u32[]{:S(2)}) copy-start(bf16[16,16,1152]{2,1,0:T(8,128)(2,1)} %param.12) | copy-start | bytes 1769476
  10.9 29.1 %collective-permute-start = (bf16[4,8,16,1152]{3,2,1,0:T(8,128)(2,1)}, bf16[4,8,16,1152]{3,2,1,0:T(8,128)(2,1)}, u32[]{:S(2)}, u32[]{:S(2)}) collective-permute-start(bf16[4,8,16,1152]{3,2,1,0:T(8,128)(2,1)} %get-tuple-element.265), channel_id=1, source_target_pairs={{0,16},{16,32},{32,48},{48,64},{64,80},{80,96},{96,112},{112,128},... | collective-permute-start | bytes 3538952 | tf_op jit(solution)/shard_map/ppermute | solution.py:19
  15.4 29.6 %collective-permute-start.1 = (bf16[4,8,16,1152]{3,2,1,0:T(8,128)(2,1)}, bf16[4,8,16,1152]{3,2,1,0:T(8,128)(2,1)}, u32[]{:S(2)}, u32[]{:S(2)}) collective-permute-start(bf16[4,8,16,1152]{3,2,1,0:T(8,128)(2,1)} %get-tuple-element.266), channel_id=1, source_target_pairs={{16,0},{32,16},{48,32},{64,48},{80,64},{96,80},{112,96},{128,112},... | collective-permute-start | bytes 3538952 | tf_op jit(solution)/shard_map/ppermute | solution.py:21
  50.5 30.5 %collective-permute-start.2 = (bf16[4,32,8,1152]{3,2,1,0:T(8,128)(2,1)}, bf16[4,32,8,1152]{3,2,1,0:T(8,128)(2,1)}, u32[]{:S(2)}, u32[]{:S(2)}) collective-permute-start(bf16[4,32,8,1152]{3,2,1,0:T(8,128)(2,1)} %get-tuple-element.263), channel_id=1, source_target_pairs={{0,1},{1,2},{2,3},{3,4},{4,5},{5,6},{6,7},{7,8},{8,9},{9,10},{10,1... | collective-permute-start | bytes 7077896 | tf_op jit(solution)/shard_map/ppermute | solution.py:19
  52.5 5.9 %copy-start.10 = (f32[4,4]{1,0:T(4,128)S(1)}, f32[4,4]{1,0:T(4,128)}, u32[]{:S(2)}) copy-start(f32[4,4]{1,0:T(4,128)} %param.17) | copy-start | bytes 196
  52.5 30.4 %collective-permute-start.3 = (bf16[4,32,8,1152]{3,2,1,0:T(8,128)(2,1)}, bf16[4,32,8,1152]{3,2,1,0:T(8,128)(2,1)}, u32[]{:S(2)}, u32[]{:S(2)}) collective-permute-start(bf16[4,32,8,1152]{3,2,1,0:T(8,128)(2,1)} %get-tuple-element.264), channel_id=1, source_target_pairs={{1,0},{2,1},{3,2},{4,3},{5,4},{6,5},{7,6},{8,7},{9,8},{10,9},{11,1... | collective-permute-start | bytes 7077896 | tf_op jit(solution)/shard_map/ppermute | solution.py:21
  62.1 14.7 %copy-start.7 = (bf16[4,16,1152]{2,1,0:T(8,128)(2,1)}, bf16[4,16,1152]{2,1,0:T(8,128)(2,1)S(1)}, u32[]{:S(2)}) copy-start(bf16[4,16,1152]{2,1,0:T(8,128)(2,1)S(1)} %reshape.226) | copy-start | bytes 442372
  62.1 9.1 %collective-permute-start.4 = (bf16[4,16,1152]{2,1,0:T(8,128)(2,1)S(1)}, bf16[4,16,1152]{2,1,0:T(8,128)(2,1)S(1)}, u32[]{:S(2)}, u32[]{:S(2)}) collective-permute-start(bf16[4,16,1152]{2,1,0:T(8,128)(2,1)S(1)} %reshape.226), channel_id=1, source_target_pairs={{0,16},{16,0},{32,48},{48,32},{64,80},{80,64},{96,112},{112,96},{1... | collective-permute-start | bytes 442376 | tf_op jit(solution)/shard_map/ppermute | solution.py:35
  71.2 5.6 %copy-start.8 = (bf16[4,16,1152]{2,1,0:T(8,128)(2,1)}, bf16[4,16,1152]{2,1,0:T(8,128)(2,1)S(1)}, u32[]{:S(2)}) copy-start(bf16[4,16,1152]{2,1,0:T(8,128)(2,1)S(1)} %collective-permute-done.4) | copy-start | bytes 442372
  71.2 5.6 %collective-permute-start.5 = (bf16[4,32,1152]{2,1,0:T(8,128)(2,1)S(1)}, bf16[4,32,1152]{2,1,0:T(8,128)(2,1)}, u32[]{:S(2)}, u32[]{:S(2)}) collective-permute-start(bf16[4,32,1152]{2,1,0:T(8,128)(2,1)S(1)} %pad_maximum_fusion.8), channel_id=1, source_target_pairs={{0,1},{1,0},{2,3},{3,2},{4,5},{5,4},{6,7},{7,6},{8,9},{9,8},{10,11... | collective-permute-start | bytes 884744 | tf_op jit(solution)/shard_map/ppermute | solution.py:35
  105.3 235.0 %copy-start.9 = (f32[2,16]{1,0:T(2,128)S(1)}, f32[2,16]{1,0:T(2,128)}, u32[]{:S(2)}) copy-start(f32[2,16]{1,0:T(2,128)} %param.19) | copy-start | bytes 388
  342.6 5.1 %copy-start.2 = (bf16[4,1024,1152]{1,2,0:T(8,128)(2,1)S(1)}, bf16[4,1024,1152]{1,2,0:T(8,128)(2,1)}, u32[]{:S(2)}) copy-start(bf16[4,1024,1152]{1,2,0:T(8,128)(2,1)} %get-tuple-element.439) | copy-start | bytes 28311556 | tf_op jit(solution)/shard_map/while
  358.7 5.1 %copy-start.2 = (bf16[4,1024,1152]{1,2,0:T(8,128)(2,1)S(1)}, bf16[4,1024,1152]{1,2,0:T(8,128)(2,1)}, u32[]{:S(2)}) copy-start(bf16[4,1024,1152]{1,2,0:T(8,128)(2,1)} %get-tuple-element.439) | copy-start | bytes 28311556 | tf_op jit(solution)/shard_map/while
  374.9 5.1 %copy-start.2 = (bf16[4,1024,1152]{1,2,0:T(8,128)(2,1)S(1)}, bf16[4,1024,1152]{1,2,0:T(8,128)(2,1)}, u32[]{:S(2)}) copy-start(bf16[4,1024,1152]{1,2,0:T(8,128)(2,1)} %get-tuple-element.439) | copy-start | bytes 28311556 | tf_op jit(solution)/shard_map/while
  391.0 5.1 %copy-start.2 = (bf16[4,1024,1152]{1,2,0:T(8,128)(2,1)S(1)}, bf16[4,1024,1152]{1,2,0:T(8,128)(2,1)}, u32[]{:S(2)}) copy-start(bf16[4,1024,1152]{1,2,0:T(8,128)(2,1)} %get-tuple-element.439) | copy-start | bytes 28311556 | tf_op jit(solution)/shard_map/while
  407.2 5.1 %copy-start.2 = (bf16[4,1024,1152]{1,2,0:T(8,128)(2,1)S(1)}, bf16[4,1024,1152]{1,2,0:T(8,128)(2,1)}, u32[]{:S(2)}) copy-start(bf16[4,1024,1152]{1,2,0:T(8,128)(2,1)} %get-tuple-element.439) | copy-start | bytes 28311556 | tf_op jit(solution)/shard_map/while
  423.3 5.1 %copy-start.2 = (bf16[4,1024,1152]{1,2,0:T(8,128)(2,1)S(1)}, bf16[4,1024,1152]{1,2,0:T(8,128)(2,1)}, u32[]{:S(2)}) copy-start(bf16[4,1024,1152]{1,2,0:T(8,128)(2,1)} %get-tuple-element.439) | copy-start | bytes 28311556 | tf_op jit(solution)/shard_map/while
  439.5 5.1 %copy-start.2 = (bf16[4,1024,1152]{1,2,0:T(8,128)(2,1)S(1)}, bf16[4,1024,1152]{1,2,0:T(8,128)(2,1)}, u32[]{:S(2)}) copy-start(bf16[4,1024,1152]{1,2,0:T(8,128)(2,1)} %get-tuple-element.439) | copy-start | bytes 28311556 | tf_op jit(solution)/shard_map/while
  455.6 5.1 %copy-start.2 = (bf16[4,1024,1152]{1,2,0:T(8,128)(2,1)S(1)}, bf16[4,1024,1152]{1,2,0:T(8,128)(2,1)}, u32[]{:S(2)}) copy-start(bf16[4,1024,1152]{1,2,0:T(8,128)(2,1)} %get-tuple-element.439) | copy-start | bytes 28311556 | tf_op jit(solution)/shard_map/while
  469.5 2.1 copy-start.1
Sparse Core Ops, SparseCore 0:
  39.8 293.6 all-gather.2
where the time goes:
time: 480 us; the launch traced here: 478 us
  waiting for transfers between devices  243 us (51%)
  local copies, waits for them, and re-layouts  90.3 us (19%)
  matrix products  63.8 us (13%)
  other arithmetic  26.1 us (5%)
  blocking collectives  21.2 us (4%)
  starting transfers between devices  18.3 us (4%)
  between operations  14.3 us (3%)
    all_gather x1, waiting for transfers between devices, body(): far_keys = lax.all_gather(col_done, 'row', axis=1, tiled=True)  228 us
    slice x16, local copies, waits for them, and re-layouts, pair_step(): valtan_parts.append(columns(block[3]).reshape(count, 2, head_dim))  30.8 us
    unnamed x25, local copies, waits for them, and re-layouts  23.5 us
    all_gather x1, blocking collectives, body(): col_done = lax.all_gather(far_local, 'col', axis=1, tiled=True)  21.2 us
    dot_general x24, matrix products, pair_step(): jnp.einsum('qhd,khd->hqk', query_pair, keytan_part, preferred_element_typ...  14.7 us
    concatenate x2, other arithmetic, with_halo(): jnp.concatenate([lax.ppermute(tail, axis, [(i, (i + 1) % count) for i in...  12.6 us
    dynamic_slice x112, local copies, waits for them, and re-layouts, columns(): return lax.dynamic_slice_in_dim(array, start, pair_width, array.ndim - 1)  11.6 us
    while x16, local copies, waits for them, and re-layouts  11 us
  transfers between devices with their start and end apart: 7, of which 6 were waited for; matrix products, arithmetic and copies ran while one was open for 8% of the time, Pallas kernels for 0%

commit v1 on v0

--- a/solution.py
+++ b/solution.py
@@ -6,6 +6,11 @@
 HEADS = 16
 RIM = 8
 NEAR_POOL = 4
+
+
+def exchange_gather(x, name, dim):
+    stack = jnp.stack([x] * lax.axis_size(name))
+    return jnp.concatenate(lax.all_to_all(stack, name, 0, 0), axis=dim)
 
 
 def with_halo(cells, sides, width):
@@ -69,7 +74,7 @@
     near_keys = jnp.concatenate([near_pair, partner(near_pair, "col", 0)], axis=1)
     far_local = pool_stack(stacked_wide, pool_far, window)
     col_done = lax.all_gather(far_local, "col", axis=1, tiled=True)
-    far_keys = lax.all_gather(col_done, "row", axis=1, tiled=True)
+    far_keys = exchange_gather(col_done, "row", 1)
     row_ids = lax.axis_index("row") * window - RIM + jnp.arange(span, dtype=jnp.int32)
     col_ids = lax.axis_index("col") * window - RIM + jnp.arange(span, dtype=jnp.int32)
     row_ok = (row_ids >= 0) & (row_ids < window * lax.axis_size("row"))

time: 480 us -> 576 us (1.20)
  the two profiles are of different devices: /device:TPU:96 before, /device:TPU:137 now
where the time goes in v1:
time: 576 us; the launch traced here: 575 us
  starting transfers between devices  249 us (43%)
  waiting for transfers between devices  110 us (19%)
  local copies, waits for them, and re-layouts  105 us (18%)
  matrix products  64.1 us (11%)
  other arithmetic  24.1 us (4%)
  blocking collectives  20.2 us (4%)
    ppermute x2, starting transfers between devices, with_halo(): lax.ppermute(tail, axis, [(i, (i + 1) % count) for i in range(ends)])  216 us
    ppermute x2, waiting for transfers between devices, with_halo(): lax.ppermute(tail, axis, [(i, (i + 1) % count) for i in range(ends)])  96.5 us
    slice x16, local copies, waits for them, and re-layouts, pair_step(): valtan_parts.append(columns(block[3]).reshape(count, 2, head_dim))  30.8 us
    unnamed x31, local copies, waits for them, and re-layouts  23.6 us
    all_gather x1, blocking collectives, body(): col_done = lax.all_gather(far_local, 'col', axis=1, tiled=True)  20.2 us
    dynamic_slice x112, local copies, waits for them, and re-layouts, columns(): return lax.dynamic_slice_in_dim(array, start, pair_width, array.ndim - 1)  18.7 us
    ppermute x2, starting transfers between devices, with_halo(): lax.ppermute(head, axis, [((i + 1) % count, i) for i in range(ends)])  15.8 us
    dot_general x24, matrix products, pair_step(): jnp.einsum('qhd,khd->hqk', query_pair, keytan_part, preferred_element_typ...  14.7 us
  transfers between devices with their start and end apart: 7, of which 5 were waited for; matrix products, arithmetic and copies ran while one was open for 6% of the time, Pallas kernels for 0%

profile of v1, /device:TPU:137, one launch (start us, length us, event | category | flops | bytes accessed | tf_op | source)
XLA Modules:
  0.0 574.7 jit_solution(12442402790773903179)
XLA Ops:
  0.6 2.0 pad_maximum_fusion.2
  3.7 20.2 %all-gather = bf16[4,18432]{1,0:T(4,128)(2,1)S(1)} all-gather(bf16[4,1152]{1,0:T(4,128)(2,1)S(1)} %bitcast.214), channel_id=2, replica_groups=mesh['row'=32,'col'=16] {'col'}, dimensions={1}, use_global_device_ids=true | all-gather | bytes 156672 | tf_op jit(solution)/shard_map/all_gather | solution.py:76
  24.0 2.8 stack.32
  26.7 12.8 %all-to-all-start = ((bf16[32,4,16,1152]{3,2,1,0:T(8,128)(2,1)}), bf16[32,4,16,1152]{3,2,1,0:T(8,128)(2,1)}, u32[]{:S(2)}, u32[]{:S(2)}) async-start(bf16[32,4,16,1152]{3,2,1,0:T(8,128)(2,1)} %stack.32), calls=%async_computation | async-start | bytes 9437184 | tf_op jit(solution)/shard_map/all_to_all | solution.py:13
  39.8 3.2 collective-permute-start
  43.0 13.9 %collective-permute-start.1 = (bf16[4,8,16,1152]{3,2,1,0:T(8,128)(2,1)S(1)}, bf16[4,8,16,1152]{3,2,1,0:T(8,128)(2,1)S(1)}, u32[]{:S(2)}, u32[]{:S(2)}) collective-permute-start(bf16[4,8,16,1152]{3,2,1,0:T(8,128)(2,1)S(1)} %get-tuple-element.277), channel_id=1, source_target_pairs={{16,0},{32,16},{48,32},{64,48},{80,64},{96,80},{112,96},{128,112},... | collective-permute-start | bytes 3538952 | tf_op jit(solution)/shard_map/ppermute | solution.py:26
  56.9 91.9 %collective-permute-done = bf16[4,8,16,1152]{3,2,1,0:T(8,128)(2,1)S(1)} collective-permute-done((bf16[4,8,16,1152]{3,2,1,0:T(8,128)(2,1)S(1)}, bf16[4,8,16,1152]{3,2,1,0:T(8,128)(2,1)S(1)}, u32[]{:S(2)}, u32[]{:S(2)}) %collective-permute-start) | collective-permute-done | bytes 1179680 | tf_op jit(solution)/shard_map/ppermute | solution.py:24
  148.8 5.1 collective-permute-done.1
  155.9 2.6 fusion.55
  158.5 213.0 %collective-permute-start.2 = (bf16[4,32,8,1152]{3,2,1,0:T(8,128)(2,1)}, bf16[4,32,8,1152]{3,2,1,0:T(8,128)(2,1)}, u32[]{:S(2)}, u32[]{:S(2)}) collective-permute-start(bf16[4,32,8,1152]{3,2,1,0:T(8,128)(2,1)} %get-tuple-element.274), channel_id=1, source_target_pairs={{0,1},{1,2},{2,3},{3,4},{4,5},{5,6},{6,7},{7,8},{8,9},{9,10},{10,1... | collective-permute-start | bytes 7077896 | tf_op jit(solution)/shard_map/ppermute | solution.py:24
  371.5 1.9 collective-permute-start.3
  376.5 3.7 fusion.44
  380.4 1.9 collective-permute-start.4
  382.3 4.4 collective-permute-done.4
  386.7 2.1 collective-permute-start.5
  389.9 2.1 copy.38
  393.1 4.6 collective-permute-done.2
  397.6 4.4 collective-permute-done.3
  402.0 9.9 %pad_maximum_fusion = bf16[4,32,32,1152]{3,2,1,0:T(8,128)(2,1)} fusion(bf16[4,32,8,1152]{3,2,1,0:T(8,128)(2,1)} %collective-permute-done.3, bf16[4,8,16,1152]{3,2,1,0:T(8,128)(2,1)} %copy-done.10, bf16[1,16,16,1152]{3,2,1,0:T(8,128)(2,1)S(1)} %bitcast.192, bf16[1,16,16,1152]{3,2,1,0:T(8,128)(2,1)S(1)} %bitcast.195, ...), kind=kLoop, calls=%fused_computation.75 | loop fusion | flops 75497472 | bytes 18874368 | tf_op jit(solution)/shard_map/concatenate | solution.py:22
  411.9 12.7 %copy.35 = bf16[4,1024,1152]{1,2,0:T(8,128)(2,1)} copy(bf16[4,1024,1152]{2,1,0:T(8,128)(2,1)} %bitcast.172) | data formatting | bytes 18874368
  424.6 4.9 copy.34
  429.5 6.7 %copy.37 = bf16[4,512,1152]{1,2,0:T(8,128)(2,1)} copy(bf16[4,512,1152]{2,1,0:T(8,128)(2,1)} %bitcast.188) | data formatting | bytes 9437184
  436.2 136.3 %while.16 = (s32[]{:T(128)}, bf16[256,1152]{0,1:T(8,128)(2,1)S(1)}, bf16[256,1152]{0,1:T(8,128)(2,1)S(1)}, bf16[4,1024,1152]{1,2,0:T(8,128)(2,1)}, bf16[256,1152...) while((s32[]{:T(128)}, bf16[256,1152]{0,1:T(8,128)(2,1)S(1)}, ...), condition=%wide.region_10.11_spmd.clone, body=%wide.region_0.10_spmd.clone.sunk | while | flops 726347264 | bytes 104430016 | solution.py:161
  439.4 2.8 fusion.181
  443.1 1.4 copy-done.2
  456.4 2.8 fusion.181
  473.5 2.8 fusion.181
  490.5 2.8 fusion.181
  507.5 2.8 fusion.181
  524.6 2.8 fusion.181
  541.6 2.8 fusion.181
  558.7 2.8 fusion.181
  (462 shorter events, 121.6 us)
Async XLA Ops:
  0.6 2.0 copy-start
  26.7 397.8 %all-to-all-start = ((bf16[32,4,16,1152]{3,2,1,0:T(8,128)(2,1)}), bf16[32,4,16,1152]{3,2,1,0:T(8,128)(2,1)}, u32[]{:S(2)}, u32[]{:S(2)}) async-start(bf16[32,4,16,1152]{3,2,1,0:T(8,128)(2,1)} %stack.32), calls=%async_computation | async-start | bytes 9437184 | tf_op jit(solution)/shard_map/all_to_all | solution.py:13
  39.5 115.4 %copy-start.3 = (bf16[16,16,1152]{2,1,0:T(8,128)(2,1)S(1)}, bf16[16,16,1152]{2,1,0:T(8,128)(2,1)}, u32[]{:S(2)}) copy-start(bf16[16,16,1152]{2,1,0:T(8,128)(2,1)} %param.16) | copy-start | bytes 1769476
  39.5 115.4 %copy-start.4 = (bf16[16,16,1152]{2,1,0:T(8,128)(2,1)S(1)}, bf16[16,16,1152]{2,1,0:T(8,128)(2,1)}, u32[]{:S(2)}) copy-start(bf16[16,16,1152]{2,1,0:T(8,128)(2,1)} %param.15) | copy-start | bytes 1769476
  39.6 115.4 %copy-start.5 = (bf16[16,16,1152]{2,1,0:T(8,128)(2,1)S(1)}, bf16[16,16,1152]{2,1,0:T(8,128)(2,1)}, u32[]{:S(2)}) copy-start(bf16[16,16,1152]{2,1,0:T(8,128)(2,1)} %param.13) | copy-start | bytes 1769476
  39.6 115.4 %copy-start.7 = (bf16[16,16,1152]{2,1,0:T(8,128)(2,1)S(1)}, bf16[16,16,1152]{2,1,0:T(8,128)(2,1)}, u32[]{:S(2)}) copy-start(bf16[16,16,1152]{2,1,0:T(8,128)(2,1)} %param.12) | copy-start | bytes 1769476
  39.8 109.1 %collective-permute-start = (bf16[4,8,16,1152]{3,2,1,0:T(8,128)(2,1)S(1)}, bf16[4,8,16,1152]{3,2,1,0:T(8,128)(2,1)S(1)}, u32[]{:S(2)}, u32[]{:S(2)}) collective-permute-start(bf16[4,8,16,1152]{3,2,1,0:T(8,128)(2,1)S(1)} %get-tuple-element.276), channel_id=1, source_target_pairs={{0,16},{16,32},{32,48},{48,64},{64,80},{80,96},{96,112},{112,128},... | collective-permute-start | bytes 3538952 | tf_op jit(solution)/shard_map/ppermute | solution.py:24
  43.0 110.9 %collective-permute-start.1 = (bf16[4,8,16,1152]{3,2,1,0:T(8,128)(2,1)S(1)}, bf16[4,8,16,1152]{3,2,1,0:T(8,128)(2,1)S(1)}, u32[]{:S(2)}, u32[]{:S(2)}) collective-permute-start(bf16[4,8,16,1152]{3,2,1,0:T(8,128)(2,1)S(1)} %get-tuple-element.277), channel_id=1, source_target_pairs={{16,0},{32,16},{48,32},{64,48},{80,64},{96,80},{112,96},{128,112},... | collective-permute-start | bytes 3538952 | tf_op jit(solution)/shard_map/ppermute | solution.py:26
  148.8 5.1 copy-start.9
  153.9 1.0 copy-start.10
  155.9 217.6 %copy-start.8 = (bf16[16,16,1152]{2,1,0:T(8,128)(2,1)S(1)}, bf16[16,16,1152]{2,1,0:T(8,128)(2,1)}, u32[]{:S(2)}) copy-start(bf16[16,16,1152]{2,1,0:T(8,128)(2,1)} %param.12) | copy-start | bytes 1769476
  155.9 217.8 %copy-start.6 = (bf16[16,16,1152]{2,1,0:T(8,128)(2,1)S(1)}, bf16[16,16,1152]{2,1,0:T(8,128)(2,1)}, u32[]{:S(2)}) copy-start(bf16[16,16,1152]{2,1,0:T(8,128)(2,1)} %param.13) | copy-start | bytes 1769476
  158.5 239.1 %collective-permute-start.2 = (bf16[4,32,8,1152]{3,2,1,0:T(8,128)(2,1)}, bf16[4,32,8,1152]{3,2,1,0:T(8,128)(2,1)}, u32[]{:S(2)}, u32[]{:S(2)}) collective-permute-start(bf16[4,32,8,1152]{3,2,1,0:T(8,128)(2,1)} %get-tuple-element.274), channel_id=1, source_target_pairs={{0,1},{1,2},{2,3},{3,4},{4,5},{5,6},{6,7},{7,8},{8,9},{9,10},{10,1... | collective-permute-start | bytes 7077896 | tf_op jit(solution)/shard_map/ppermute | solution.py:24
  371.5 5.0 copy-start.13
  371.5 30.5 %collective-permute-start.3 = (bf16[4,32,8,1152]{3,2,1,0:T(8,128)(2,1)}, bf16[4,32,8,1152]{3,2,1,0:T(8,128)(2,1)}, u32[]{:S(2)}, u32[]{:S(2)}) collective-permute-start(bf16[4,32,8,1152]{3,2,1,0:T(8,128)(2,1)} %get-tuple-element.275), channel_id=1, source_target_pairs={{1,0},{2,1},{3,2},{4,3},{5,4},{6,5},{7,6},{8,7},{9,8},{10,9},{11,1... | collective-permute-start | bytes 7077896 | tf_op jit(solution)/shard_map/ppermute | solution.py:26
  376.5 12.3 %copy-start.11 = (bf16[16,16,1152]{2,1,0:T(8,128)(2,1)S(1)}, bf16[16,16,1152]{2,1,0:T(8,128)(2,1)}, u32[]{:S(2)}) copy-start(bf16[16,16,1152]{2,1,0:T(8,128)(2,1)} %param.11) | copy-start | bytes 1769476
  380.4 6.3 %collective-permute-start.4 = (bf16[4,16,1152]{2,1,0:T(8,128)(2,1)S(1)}, bf16[4,16,1152]{2,1,0:T(8,128)(2,1)S(1)}, u32[]{:S(2)}, u32[]{:S(2)}) collective-permute-start(bf16[4,16,1152]{2,1,0:T(8,128)(2,1)S(1)} %reshape.234), channel_id=1, source_target_pairs={{0,16},{16,0},{32,48},{48,32},{64,80},{80,64},{96,112},{112,96},{1... | collective-permute-start | bytes 442376 | tf_op jit(solution)/shard_map/ppermute | solution.py:40
  386.7 5.3 collective-permute-start.5
  429.4 6.8 %copy-start.12 = (f32[2,16]{1,0:T(2,128)S(1)}, f32[2,16]{1,0:T(2,128)}, u32[]{:S(2)}) copy-start(f32[2,16]{1,0:T(2,128)} %param.19) | copy-start | bytes 388
  439.4 5.1 copy-start.2
  456.4 5.1 copy-start.2
  473.5 5.1 copy-start.2
  490.5 5.1 copy-start.2
  507.5 5.1 copy-start.2
  524.6 5.1 copy-start.2
  541.6 5.1 copy-start.2
  558.7 5.1 copy-start.2
  572.6 2.1 copy-start.1
